TPU v7x, 32 devices: a whole 2x2x4 slice. The times are simulated.
32 devices in a mesh: dp: 8 (over z, x), head: 4 (over y, core).
Axes of the slice: x: 2, y: 2, z: 4, core: 2. Of those that a mesh axis runs over, the one named last changes fastest.
Arguments:
- vit_ctx: bfloat16 [1024, 1536], P('dp', 'head'), may hold values from -6 to 6
- vit_resid: bfloat16 [1024, 1600], P('dp'), may hold values from -6 to 6
- vit_proj: bfloat16 [4, 384, 1600], P('head', 'dp'), may hold values from -0.15625 to 0.15625
- vit_grad: bfloat16 [1024, 1600], P('dp'), may hold values from -6 to 6
- norm_gain: float32 [1600], replicated, may hold values from 0.1 to 1.9
- cross_q: bfloat16 [96, 2048], P(None, 'head'), may hold values from -400 to 400
- key_w: bfloat16 [1600, 2048], P(None, 'head'), may hold values from -0.15625 to 0.15625
- value_w: bfloat16 [1600, 2048], P(None, 'head'), may hold values from -0.15625 to 0.15625
- out_w: bfloat16 [2048, 4096], P('head'), may hold values from -0.125 to 0.125
- query_state: bfloat16 [96, 4096], P(None, 'head'), may hold values from -1.5 to 1.5
Outputs:
- ctx_grad: bfloat16 [1024, 1536], P('dp', 'head')
- proj_grad: float32 [4, 384, 1600], P('head', 'dp')
- cross_out: bfloat16 [8, 96, 4096], P('dp', None, 'head')
All inputs are finite; a program needn't handle non-finite values.
Results may differ from a plain program's by a relative error of at most 0.017.
The roundings to bfloat16 on the way count: a program that leaves them out, or rounds other values in their place, can miss the bound.
Values may be sent and summed in bfloat16 or wider, within the bound.
A program may use at most 64 MiB of HBM per device.

v0:
```python
import math
import jax
import jax.numpy as jnp
from jax import lax
from jax.sharding import PartitionSpec as P

HD = 128
EPSILON = 1e-06


def on_device(
    vit_ctx, vit_resid, vit_proj, vit_grad, norm_gain, cross_q, key_w, value_w, out_w, query_state
):
    contract_cols = (((1,), (1,)), ((), ()))
    ctx_part = vit_ctx
    partial_value = jnp.dot(
        ctx_part,
        lax.all_gather(vit_proj, "dp", axis=1, tiled=True)[0],
        preferred_element_type=jnp.float32,
    )
    ctx_grad = lax.dot_general(
        vit_grad,
        lax.all_gather(vit_proj, "dp", axis=1, tiled=True)[0],
        contract_cols,
        preferred_element_type=jnp.float32,
    ).astype(jnp.bfloat16)
    ctx_part = vit_ctx
    grad_share = lax.psum_scatter(
        lax.dot_general(
            ctx_part, vit_grad, (((0,), (0,)), ((), ())), preferred_element_type=jnp.float32
        ),
        "dp",
        scatter_dimension=0,
        tiled=True,
    )
    proj_grad = grad_share[None]
    feature_count = partial_value.shape[1]
    summed = lax.psum(partial_value, "head")
    hidden = vit_resid.astype(jnp.float32) + summed
    row_mean = jnp.sum(hidden, axis=1, keepdims=True) / feature_count
    square_mean = jnp.sum(hidden * hidden, axis=1, keepdims=True) / feature_count
    variance = square_mean - row_mean * row_mean
    features = ((hidden - row_mean) * lax.rsqrt(variance + EPSILON) * norm_gain).astype(
        jnp.bfloat16
    )
    head_count = key_w.shape[1] // HD
    query_count = cross_q.shape[0]
    key_rows = jnp.dot(features, key_w, preferred_element_type=jnp.float32).astype(jnp.bfloat16)
    value_rows = jnp.dot(features, value_w, preferred_element_type=jnp.float32).astype(jnp.bfloat16)
    queries = cross_q.reshape(query_count, head_count, HD)
    key_heads = key_rows.reshape(-1, head_count, HD)
    value_heads = value_rows.reshape(-1, head_count, HD)
    score_scale = 1.0 / math.sqrt(HD)
    scores = (
        jnp.einsum("qhd,khd->hqk", queries, key_heads, preferred_element_type=jnp.float32)
        * score_scale
    )
    row_max = jnp.max(scores, axis=2, keepdims=True)
    exponent = jnp.exp(scores - row_max)
    attn_probs = (exponent / jnp.sum(exponent, axis=2, keepdims=True)).astype(jnp.bfloat16)
    attended = jnp.einsum(
        "hqk,khd->qhd", attn_probs, value_heads, preferred_element_type=jnp.float32
    )
    attended = attended.astype(jnp.bfloat16).reshape(query_count, head_count * HD)
    out_partial = jnp.dot(attended, out_w, preferred_element_type=jnp.float32)
    out_share = lax.psum_scatter(
        out_partial.astype(jnp.bfloat16), "head", scatter_dimension=1, tiled=True
    ).astype(jnp.float32)
    cross_out = (out_share + query_state.astype(jnp.float32)).astype(jnp.bfloat16)[None]
    return (ctx_grad, proj_grad, cross_out)


def solution(mesh):
    return jax.shard_map(
        on_device,
        mesh=mesh,
        in_specs=(
            P("dp", "head"),
            P("dp", None),
            P("head", "dp", None),
            P("dp", None),
            P(),
            P(None, "head"),
            P(None, "head"),
            P(None, "head"),
            P("head", None),
            P(None, "head"),
        ),
        out_specs=(P("dp", "head"), P("head", "dp", None), P("dp", None, "head")),
        check_vma=False,
    )
```

profile of v0, /device:TPU:0, one launch (start us, length us, event | category | flops | bytes accessed | tf_op | source)
XLA Modules:
  0.0 205.2 jit_solution(9115707101834075549)
XLA Ops:
  7.2 0.0 copy-start
  7.2 0.0 all-gather.2.cloned.1.call-start
  7.2 0.7 all-gather.2.cloned.1.call-update
  7.9 0.0 copy-start.9
  7.9 0.0 all-reduce.2.cloned.1.call-start
  8.0 46.6 %all-gather.2.cloned.1.call-done = bf16[1,384,1600]{2,1,0:T(8,128)(2,1)} async-done(((bf16[1,48,1600]{2,1,0:T(8,128)(2,1)}), bf16[1,384,1600]{2,1,0:T(8,128)(2,1)}) %all-gather.2.cloned.1.call-update) | async-done | bytes 1228816 | tf_op jit(solution)/shard_map/all_gather | solution.py:23
  54.6 2.9 %fusion.1 = f32[128,1600]{0,1:T(8,128)} fusion(bf16[128,384]{1,0:T(8,128)(2,1)} %param.10, bf16[1,384,1600]{2,1,0:T(8,128)(2,1)} %all-gather.2.cloned.1.call-done), kind=kOutput, calls=%fused_computation.2 | convolution fusion | flops 157286400 | bytes 2146304 | tf_op jit(solution)/shard_map/dot_general | solution.py:16
  57.5 0.0 all-reduce.2.cloned.1.call-update
  57.5 0.0 reduce-scatter.5.cloned.1.call-start
  57.6 34.2 %all-reduce.2.cloned.1.call-done = f32[128,1600]{0,1:T(8,128)} async-done(((f32[128,1600]{0,1:T(8,128)}), f32[128,1600]{0,1:T(8,128)}) %all-reduce.2.cloned.1.call-update) | async-done | bytes 819216 | tf_op jit(solution)/shard_map/psum | solution.py:38
  91.8 0.0 copy-done.5
  91.8 1.4 fusion.14
  93.3 0.0 copy-start.4
  93.3 0.3 multiply_convert_fusion
  93.6 0.0 copy-start.8
  93.6 0.4 fusion.12
  94.1 0.7 copy-done.4
  94.7 0.4 fusion.11
  95.2 0.2 fusion.6
  95.4 0.2 fusion.26
  95.6 0.7 fusion.13
  96.4 0.0 copy-start.6
  96.4 3.9 %convolution_convert_fusion = bf16[96,4096]{1,0:T(8,128)(2,1)} fusion(bf16[512,4096]{1,0:T(8,128)(2,1)} %param.18, bf16[4,12,8,128]{3,2,1,0:T(8,128)(2,1)S(1)} %fusion.13), kind=kOutput, calls=%fused_computation.1 | convolution fusion | flops 403046400 | bytes 5079040 | tf_op jit(solution)/shard_map/dot_general | solution.py:65
  100.3 0.0 reduce-scatter.5.cloned.1.call-update
  100.3 0.0 reduce-scatter.3.cloned.1.call-start
  100.4 2.0 fusion.27
  102.4 0.0 reduce-scatter.3.cloned.1.call-update
  102.4 1.3 copy-done.1
  103.7 1.2 fusion.8
  104.8 18.8 %reduce-scatter.5.cloned.1.call-done = bf16[96,1024]{1,0:T(8,128)(2,1)} async-done(((bf16[96,4096]{1,0:T(8,128)(2,1)}), bf16[96,1024]{1,0:T(8,128)(2,1)}) %reduce-scatter.5.cloned.1.call-update) | async-done | bytes 196624 | tf_op jit(solution)/shard_map/reduce_scatter | solution.py:66
  123.7 1.7 fusion.15
  125.3 73.4 %reduce-scatter.3.cloned.1.call-done = f32[48,1600]{1,0:T(8,128)} async-done(((f32[384,1600]{1,0:T(8,128)}), f32[48,1600]{1,0:T(8,128)}) %reduce-scatter.3.cloned.1.call-update) | async-done | bytes 307216 | tf_op jit(solution)/shard_map/reduce_scatter | solution.py:28
  (13 shorter events, 0.0 us)
Async XLA Ops:
  7.2 86.4 %copy-start = (bf16[1600,512]{1,0:T(8,128)(2,1)S(1)}, bf16[1600,512]{1,0:T(8,128)(2,1)}, u32[]{:S(2)}) copy-start(bf16[1600,512]{1,0:T(8,128)(2,1)} %param.16) | copy-start | bytes 4915204
  7.2 84.6 %copy-start.5 = (bf16[128,1600]{0,1:T(8,128)(2,1)S(1)}, bf16[128,1600]{0,1:T(8,128)(2,1)}, u32[]{:S(2)}) copy-start(bf16[128,1600]{0,1:T(8,128)(2,1)} %param.11) | copy-start | bytes 1228804
  7.2 47.4 %all-gather.2.cloned.1.call-start = ((), (), s32[]{:S(2)}) async-start(), calls=%async_computation.2 | async-start | bytes 1437696 | tf_op jit(solution)/shard_map/all_gather | solution.py:23
  7.9 85.3 %copy-start.9 = (f32[1600]{0:T(1024)S(1)}, f32[1600]{0:T(1024)}, u32[]{:S(2)}) copy-start(f32[1600]{0:T(1024)} %param.14) | copy-start | bytes 19204
  7.9 83.9 %all-reduce.2.cloned.1.call-start = ((), (), s32[]{:S(2)}) async-start(), calls=%async_computation.4 | async-start | bytes 1638400 | tf_op jit(solution)/shard_map/psum | solution.py:38
  57.5 66.1 %reduce-scatter.5.cloned.1.call-start = ((), (), s32[]{:S(2)}) async-start(), calls=%async_computation.5 | async-start | bytes 983040 | tf_op jit(solution)/shard_map/reduce_scatter | solution.py:66
  91.8 1.5 copy-start.2
  93.3 1.4 copy-start.4
  93.6 1.6 copy-start.8
  96.4 4.0 %copy-start.3 = (bf16[128,1600]{0,1:T(8,128)(2,1)S(1)}, bf16[128,1600]{0,1:T(8,128)(2,1)}, u32[]{:S(2)}) copy-start(bf16[128,1600]{0,1:T(8,128)(2,1)} %param.13) | copy-start | bytes 1228804
  96.4 4.0 %copy-start.6 = (bf16[128,384]{1,0:T(8,128)(2,1)S(1)}, bf16[128,384]{1,0:T(8,128)(2,1)}, u32[]{:S(2)}) copy-start(bf16[128,384]{1,0:T(8,128)(2,1)} %param.10) | copy-start | bytes 294916
  100.3 98.4 %reduce-scatter.3.cloned.1.call-start = ((), (), s32[]{:S(2)}) async-start(), calls=%async_computation.3 | async-start | bytes 2875392 | tf_op jit(solution)/shard_map/reduce_scatter | solution.py:28
  102.4 1.3 copy-start.1
  102.4 21.3 %copy-start.7 = (bf16[96,1024]{1,0:T(8,128)(2,1)S(1)}, bf16[96,1024]{1,0:T(8,128)(2,1)}, u32[]{:S(2)}) copy-start(bf16[96,1024]{1,0:T(8,128)(2,1)} %param.19) | copy-start | bytes 589828
Sparse Core Ops, SparseCore 0:
  10.2 44.4 all-gather.1
  57.7 34.0 all-reduce.1
  100.4 23.1 reduce-scatter.4
  127.6 71.0 reduce-scatter.2
where the time goes:
time: 205 us
  waiting for transfers between devices  174 us (85%)
  between operations  13.9 us (7%)
  matrix products  11.8 us (6%)
  other arithmetic  3.64 us (2%)
    reduce_scatter x1, waiting for transfers between devices, on_device(): lax.psum_scatter(lax.dot_general(ctx_part, vit_grad, (((0,), (0,)), ((),...  73.4 us
    all_gather x1, waiting for transfers between devices, on_device(): lax.all_gather(vit_proj, 'dp', axis=1, tiled=True)[0]  46.6 us
    psum x1, waiting for transfers between devices, on_device(): summed = lax.psum(partial_value, 'head')  34.2 us
    reduce_scatter x1, waiting for transfers between devices, on_device(): lax.psum_scatter(out_partial.astype(jnp.bfloat16), 'head', scatter_dimens...  18.8 us
  transfers between devices with their start and end apart: 4, of which 4 were waited for; matrix products, arithmetic and copies ran while one was open for 2% of the time, Pallas kernels for 0%

commit v1 on v0

--- a/solution.py
+++ b/solution.py
@@ -35,7 +35,15 @@
     )
     proj_grad = grad_share[None]
     feature_count = partial_value.shape[1]
-    summed = lax.psum(partial_value, "head")
+
+    def group_series(view):
+        q_n = lax.axis_size("head")
+        spare = view
+        for c in [[(ix, ix ^ ii) for ix in range(q_n)] for ii in (1, 2, 4, 8, 16) if ii < q_n]:
+            spare = spare + lax.ppermute(spare, axis_name="head", perm=c)
+        return spare
+
+    summed = group_series(partial_value)
     hidden = vit_resid.astype(jnp.float32) + summed
     row_mean = jnp.sum(hidden, axis=1, keepdims=True) / feature_count
     square_mean = jnp.sum(hidden * hidden, axis=1, keepdims=True) / feature_count

time: 205 us -> 191 us (0.932)
  waiting for transfers between devices: 174 us -> 160 us
    psum x1 -> x0, waiting for transfers between devices: 34.2 us -> none  [on_device(): summed = lax.psum(partial_value, 'head')]
    ppermute x0 -> x2, waiting for transfers between devices: none -> 21.1 us  [group_series(): spare = spare + lax.ppermute(spare, axis_name='head', perm=c)]
  transfers between devices with their start and end apart: 4 -> 5, of which waited for: 4 -> 5; matrix products, arithmetic and copies ran while one was open for 2% -> 3% of each run, Pallas kernels for 0% -> 0%
where the time goes in v1:
time: 191 us
  waiting for transfers between devices  160 us (84%)
  between operations  13.9 us (7%)
  matrix products  11.8 us (6%)
  other arithmetic  2.22 us (1%)
    reduce_scatter x1, waiting for transfers between devices, on_device(): lax.psum_scatter(lax.dot_general(ctx_part, vit_grad, (((0,), (0,)), ((),...  73.4 us
    all_gather x1, waiting for transfers between devices, on_device(): lax.all_gather(vit_proj, 'dp', axis=1, tiled=True)[0]  46.6 us
    ppermute x2, waiting for transfers between devices, group_series(): spare = spare + lax.ppermute(spare, axis_name='head', perm=c)  21.1 us
    reduce_scatter x1, waiting for transfers between devices, on_device(): lax.psum_scatter(out_partial.astype(jnp.bfloat16), 'head', scatter_dimens...  17.7 us
    dot_general x1, matrix products, on_device(): out_partial = jnp.dot(attended, out_w, preferred_element_type=jnp.float32)  3.92 us
  transfers between devices with their start and end apart: 5, of which 5 were waited for; matrix products, arithmetic and copies ran while one was open for 3% of the time, Pallas kernels for 0%

profile of v1, /device:TPU:0, one launch (start us, length us, event | category | flops | bytes accessed | tf_op | source)
XLA Modules:
  0.0 191.0 jit_solution(8808292167261373039)
XLA Ops:
  7.2 0.0 copy-start
  7.2 0.0 all-gather.2.cloned.1.call-start
  7.2 0.7 all-gather.2.cloned.1.call-update
  7.9 0.0 reduce-scatter.5.cloned.1.call-start
  8.0 46.6 %all-gather.2.cloned.1.call-done = bf16[1,384,1600]{2,1,0:T(8,128)(2,1)} async-done(((bf16[1,48,1600]{2,1,0:T(8,128)(2,1)}), bf16[1,384,1600]{2,1,0:T(8,128)(2,1)}) %all-gather.2.cloned.1.call-update) | async-done | bytes 1228816 | tf_op jit(solution)/shard_map/all_gather | solution.py:23
  54.6 2.0 %fusion.1 = f32[128,1600]{0,1:T(8,128)S(1)} fusion(bf16[128,384]{1,0:T(8,128)(2,1)} %param.10, bf16[1,384,1600]{2,1,0:T(8,128)(2,1)} %all-gather.2.cloned.1.call-done), kind=kOutput, calls=%fused_computation.2 | convolution fusion | flops 157286400 | bytes 2146304 | tf_op jit(solution)/shard_map/dot_general | solution.py:16
  56.6 0.0 copy-start.4
  56.6 0.1 collective-permute-start
  56.7 2.3 %collective-permute-done = f32[128,1600]{0,1:T(8,128)S(1)} collective-permute-done((f32[128,1600]{0,1:T(8,128)S(1)}, f32[128,1600]{0,1:T(8,128)S(1)}, u32[]{:S(2)}, u32[]{:S(2)}) %collective-permute-start) | collective-permute-done | bytes 819232 | tf_op jit(solution)/shard_map/ppermute | solution.py:43
  59.0 0.1 add.27
  59.1 0.0 copy-start.8
  59.1 1.5 collective-permute-start.1
  60.7 18.8 %collective-permute-done.1 = f32[128,1600]{0,1:T(8,128)S(1)} collective-permute-done((f32[128,1600]{0,1:T(8,128)S(1)}, f32[128,1600]{0,1:T(8,128)S(1)}, u32[]{:S(2)}, u32[]{:S(2)}) %collective-permute-start.1) | collective-permute-done | bytes 819232 | tf_op jit(solution)/shard_map/ppermute | solution.py:43
  79.5 0.2 fusion.25
  79.7 0.0 copy-start.3
  79.7 0.9 fusion.12
  80.7 0.5 copy-done.3
  81.1 0.9 fusion.11
  82.1 0.2 fusion.6
  82.3 0.2 fusion.26
  82.5 0.7 fusion.13
  83.2 0.0 copy-start.5
  83.3 3.9 %convolution_convert_fusion = bf16[96,4096]{1,0:T(8,128)(2,1)} fusion(bf16[512,4096]{1,0:T(8,128)(2,1)} %param.18, bf16[4,12,8,128]{3,2,1,0:T(8,128)(2,1)S(1)} %fusion.13), kind=kOutput, calls=%fused_computation.1 | convolution fusion | flops 403046400 | bytes 5079040 | tf_op jit(solution)/shard_map/dot_general | solution.py:73
  87.2 0.0 reduce-scatter.5.cloned.1.call-update
  87.2 0.0 reduce-scatter.3.cloned.1.call-start
  87.3 2.0 %fusion.27 = f32[384,1600]{1,0:T(8,128)} fusion(bf16[128,384]{1,0:T(8,128)(2,1)S(1)} %copy-done.5, bf16[128,1600]{0,1:T(8,128)(2,1)S(1)} %copy-done.2), kind=kOutput, calls=%fused_computation.37 | convolution fusion | flops 157286400 | bytes 2965504 | tf_op jit(solution)/shard_map/dot_general | solution.py:29
  89.3 0.0 reduce-scatter.3.cloned.1.call-update
  89.3 1.3 copy-done.1
  90.6 1.2 fusion.8
  91.7 17.7 %reduce-scatter.5.cloned.1.call-done = bf16[96,1024]{1,0:T(8,128)(2,1)} async-done(((bf16[96,4096]{1,0:T(8,128)(2,1)}), bf16[96,1024]{1,0:T(8,128)(2,1)}) %reduce-scatter.5.cloned.1.call-update) | async-done | bytes 196624 | tf_op jit(solution)/shard_map/reduce_scatter | solution.py:74
  109.4 1.7 fusion.14
  111.1 73.4 %reduce-scatter.3.cloned.1.call-done = f32[48,1600]{1,0:T(8,128)} async-done(((f32[384,1600]{1,0:T(8,128)}), f32[48,1600]{1,0:T(8,128)}) %reduce-scatter.3.cloned.1.call-update) | async-done | bytes 307216 | tf_op jit(solution)/shard_map/reduce_scatter | solution.py:28
  (12 shorter events, 0.0 us)
Async XLA Ops:
  7.2 72.6 %copy-start = (bf16[1600,512]{1,0:T(8,128)(2,1)S(1)}, bf16[1600,512]{1,0:T(8,128)(2,1)}, u32[]{:S(2)}) copy-start(bf16[1600,512]{1,0:T(8,128)(2,1)} %param.16) | copy-start | bytes 4915204
  7.2 47.4 %all-gather.2.cloned.1.call-start = ((), (), s32[]{:S(2)}) async-start(), calls=%async_computation.2 | async-start | bytes 1437696 | tf_op jit(solution)/shard_map/all_gather | solution.py:23
  7.9 101.5 %reduce-scatter.5.cloned.1.call-start = ((), (), s32[]{:S(2)}) async-start(), calls=%async_computation.4 | async-start | bytes 983040 | tf_op jit(solution)/shard_map/reduce_scatter | solution.py:74
  56.6 22.9 %copy-start.4 = (bf16[128,1600]{0,1:T(8,128)(2,1)S(1)}, bf16[128,1600]{0,1:T(8,128)(2,1)}, u32[]{:S(2)}) copy-start(bf16[128,1600]{0,1:T(8,128)(2,1)} %param.11) | copy-start | bytes 1228804
  56.6 2.4 %collective-permute-start = (f32[128,1600]{0,1:T(8,128)S(1)}, f32[128,1600]{0,1:T(8,128)S(1)}, u32[]{:S(2)}, u32[]{:S(2)}) collective-permute-start(f32[128,1600]{0,1:T(8,128)S(1)} %fusion.1), channel_id=1, source_target_pairs={{0,1},{1,0},{2,3},{3,2},{4,5},{5,4},{6,7},{7,6},{8,9},{9,8},{10,11... | collective-permute-start | bytes 2457608 | tf_op jit(solution)/shard_map/ppermute | solution.py:43
  59.1 20.6 %copy-start.8 = (f32[1600]{0:T(1024)S(1)}, f32[1600]{0:T(1024)}, u32[]{:S(2)}) copy-start(f32[1600]{0:T(1024)} %param.14) | copy-start | bytes 19204
  59.1 20.4 %collective-permute-start.1 = (f32[128,1600]{0,1:T(8,128)S(1)}, f32[128,1600]{0,1:T(8,128)S(1)}, u32[]{:S(2)}, u32[]{:S(2)}) collective-permute-start(f32[128,1600]{0,1:T(8,128)S(1)} %add.27), channel_id=1, source_target_pairs={{0,2},{1,3},{2,0},{3,1},{4,6},{5,7},{6,4},{7,5},{8,10},{9,11},{10,... | collective-permute-start | bytes 2457608 | tf_op jit(solution)/shard_map/ppermute | solution.py:43
  79.7 1.4 copy-start.3
  81.1 0.9 copy-start.7
  83.2 4.0 %copy-start.2 = (bf16[128,1600]{0,1:T(8,128)(2,1)S(1)}, bf16[128,1600]{0,1:T(8,128)(2,1)}, u32[]{:S(2)}) copy-start(bf16[128,1600]{0,1:T(8,128)(2,1)} %param.13) | copy-start | bytes 1228804
  83.2 4.0 %copy-start.5 = (bf16[128,384]{1,0:T(8,128)(2,1)S(1)}, bf16[128,384]{1,0:T(8,128)(2,1)}, u32[]{:S(2)}) copy-start(bf16[128,384]{1,0:T(8,128)(2,1)} %param.10) | copy-start | bytes 294916
  87.2 97.2 %reduce-scatter.3.cloned.1.call-start = ((), (), s32[]{:S(2)}) async-start(), calls=%async_computation.3 | async-start | bytes 2875392 | tf_op jit(solution)/shard_map/reduce_scatter | solution.py:28
  89.3 1.3 copy-start.1
  89.3 20.1 %copy-start.6 = (bf16[96,1024]{1,0:T(8,128)(2,1)S(1)}, bf16[96,1024]{1,0:T(8,128)(2,1)}, u32[]{:S(2)}) copy-start(bf16[96,1024]{1,0:T(8,128)(2,1)} %param.19) | copy-start | bytes 589828
Sparse Core Ops, SparseCore 0:
  10.2 44.4 all-gather.1
  87.3 22.0 reduce-scatter.4
  113.5 70.8 reduce-scatter.2
